TPU v7x, 32 devices: a whole 2x2x4 slice. The times are simulated.
32 devices in a mesh: dp: 8 (over z, core), ctx: 4 (over y, x).
Axes of the slice: x: 2, y: 2, z: 4, core: 2. Of those that a mesh axis runs over, the one named last changes fastest.
Arguments:
- queries: bfloat16 [8, 512, 1024], P('dp', 'ctx'), may hold values from -6 to 6
- key_vectors: bfloat16 [8, 512, 1024], P('dp', 'ctx'), may hold values from -6 to 6
- values: bfloat16 [8, 512, 1024], P('dp', 'ctx'), may hold values from -6 to 6
- cotangent: bfloat16 [8, 512, 1024], P('dp', 'ctx'), may hold values from -6 to 6
- lengths: int32 [8], P('dp'), may hold values from 128 to 512
- conv_taps: float32 [31, 1024], replicated, may hold values from -3 to 3
Outputs:
- conv_out: bfloat16 [8, 512, 1024], P('dp', 'ctx')
- query_grad: bfloat16 [8, 512, 1024], P('dp', 'ctx')
- key_grad: bfloat16 [8, 512, 1024], P('dp', 'ctx')
- value_grad: bfloat16 [8, 512, 1024], P('dp', 'ctx')
- taps_grad: float32 [31, 1024], replicated
All inputs are finite; a program needn't handle non-finite values.
Results may differ from a plain program's by a relative error of at most 0.024.
Values may be sent and summed in bfloat16 or wider, within the bound.
No kernel may reach another device: no remote copies, remote signals or barrier semaphores. Data moves between devices by JAX's collectives and lax.ppermute only.
A program may use at most 64 MiB of HBM per device.

v0:
```python
import jax
import jax.numpy as jnp
from jax import lax
from jax.sharding import PartitionSpec as P

HEAD_DIM = 64
KERNEL = 31


def with_halo(block, sides, width):
    for axis, dim in sides:
        count = lax.axis_size(axis)
        forward = [(i, i + 1) for i in range(count - 1)]
        backward = [(target, source) for source, target in forward]
        low = lax.ppermute(
            lax.slice_in_dim(block, block.shape[dim] - width, None, axis=dim), axis, forward
        )
        high = lax.ppermute(lax.slice_in_dim(block, 0, width, axis=dim), axis, backward)
        block = jnp.concatenate([low, block, high], axis=dim)
    return block


def attend_forward(query_heads, key_heads, value_heads, valid_keys, block_rows):
    block_count = query_heads.shape[0] // block_rows
    score_scale = HEAD_DIM ** (-0.5)

    def one_block(offset):
        query_part = lax.dynamic_slice_in_dim(query_heads, offset, block_rows, 0)
        scores = (
            jnp.einsum("qhd,khd->hqk", query_part, key_heads, preferred_element_type=jnp.float32)
            * score_scale
        )
        scores = jnp.where(valid_keys[None, None, :], scores, -1e30)
        row_top = jnp.max(scores, axis=2, keepdims=True)
        log_total = row_top + jnp.log(jnp.sum(jnp.exp(scores - row_top), axis=2, keepdims=True))
        softmax_bf = jnp.exp(scores - log_total).astype(jnp.bfloat16)
        attended = jnp.einsum(
            "hqk,khd->qhd", softmax_bf, value_heads, preferred_element_type=jnp.float32
        ).astype(jnp.bfloat16)
        return (attended, log_total[:, :, 0])

    offsets = jnp.arange(block_count, dtype=jnp.int32) * block_rows
    attended, log_totals = lax.map(one_block, offsets)
    return (attended.reshape(query_heads.shape), log_totals)


def attend_backward(
    query_heads, key_heads, value_heads, out_heads, grad_heads, log_totals, valid_keys, block_rows
):
    block_count = query_heads.shape[0] // block_rows
    score_scale = HEAD_DIM ** (-0.5)

    def one_block(carried, inputs):
        offset, log_part = inputs
        key_acc, value_acc = carried
        query_part = lax.dynamic_slice_in_dim(query_heads, offset, block_rows, 0)
        out_part = lax.dynamic_slice_in_dim(out_heads, offset, block_rows, 0)
        grad_part = lax.dynamic_slice_in_dim(grad_heads, offset, block_rows, 0)
        scores = (
            jnp.einsum("qhd,khd->hqk", query_part, key_heads, preferred_element_type=jnp.float32)
            * score_scale
        )
        scores = jnp.where(valid_keys[None, None, :], scores, -1e30)
        softmax = jnp.exp(scores - log_part[:, :, None])
        row_delta = jnp.sum(grad_part.astype(jnp.float32) * out_part.astype(jnp.float32), axis=2).T
        prob_grad = jnp.einsum(
            "qhd,khd->hqk", grad_part, value_heads, preferred_element_type=jnp.float32
        )
        score_grad = (softmax * (prob_grad - row_delta[:, :, None])).astype(jnp.bfloat16)
        query_grad = (
            jnp.einsum("hqk,khd->qhd", score_grad, key_heads, preferred_element_type=jnp.float32)
            * score_scale
        ).astype(jnp.bfloat16)
        key_acc = key_acc + jnp.einsum(
            "hqk,qhd->khd", score_grad, query_part, preferred_element_type=jnp.float32
        )
        value_acc = value_acc + jnp.einsum(
            "hqk,qhd->khd",
            softmax.astype(jnp.bfloat16),
            grad_part,
            preferred_element_type=jnp.float32,
        )
        return ((key_acc, value_acc), query_grad)

    offsets = jnp.arange(block_count, dtype=jnp.int32) * block_rows
    zeros_acc = jnp.zeros(key_heads.shape, jnp.float32)
    (key_acc, value_acc), query_grad = lax.scan(
        one_block, (zeros_acc, zeros_acc), (offsets, log_totals)
    )
    key_grad = (key_acc * score_scale).astype(jnp.bfloat16)
    return (query_grad.reshape(query_heads.shape), key_grad, value_acc.astype(jnp.bfloat16))


def conv_terms(padded_in, padded_cot, conv_taps, rows):
    half_width = KERNEL // 2
    conv_sum = jnp.zeros((rows, conv_taps.shape[1]), jnp.float32)
    back_sum = jnp.zeros((rows, conv_taps.shape[1]), jnp.float32)
    cot_rows = padded_cot[half_width : half_width + rows].astype(jnp.float32)
    tap_rows = []
    for tap_index in range(KERNEL):
        window = padded_in[tap_index : tap_index + rows]
        conv_sum = conv_sum + conv_taps[tap_index] * window
        back_sum = (
            back_sum
            + conv_taps[tap_index]
            * padded_cot[2 * half_width - tap_index : 2 * half_width - tap_index + rows]
        )
        tap_rows.append(jnp.sum(cot_rows * window, axis=0))
    return (conv_sum, back_sum, jnp.stack(tap_rows))


def split_heads(flat_rows):
    return flat_rows.reshape(flat_rows.shape[0], flat_rows.shape[1] // HEAD_DIM, HEAD_DIM)


def per_device(queries, key_vectors, values, cotangent, lengths, conv_taps):
    tok_rows = queries.shape[1]
    width = queries.shape[2]
    ctx_count = lax.axis_size("ctx")
    frames = tok_rows * ctx_count
    local_width = width // ctx_count
    block_rows = min(512, frames)
    half_width = KERNEL // 2
    length = lengths[0]
    valid_keys = jnp.arange(frames, dtype=jnp.int32) < length
    stacked = jnp.stack([queries[0], key_vectors[0], values[0]])
    exchanged = lax.all_to_all(stacked, "ctx", split_axis=2, concat_axis=1, tiled=True)
    query_heads = split_heads(exchanged[0])
    key_heads = split_heads(exchanged[1])
    value_heads = split_heads(exchanged[2])
    out_heads, log_totals = attend_forward(
        query_heads, key_heads, value_heads, valid_keys, block_rows
    )
    out_frames = lax.all_to_all(
        out_heads.reshape(frames, local_width), "ctx", split_axis=0, concat_axis=1, tiled=True
    )
    positions = lax.axis_index("ctx") * tok_rows + jnp.arange(tok_rows, dtype=jnp.int32)
    valid_rows = positions < length
    kept = jnp.where(valid_rows[:, None], out_frames, jnp.zeros_like(out_frames))
    padded_cot = with_halo(cotangent[0], (("ctx", 0),), half_width)
    padded_in = with_halo(kept, (("ctx", 0),), half_width)
    conv_sum, back_sum, taps_part = conv_terms(padded_in, padded_cot, conv_taps, tok_rows)
    conv_out = conv_sum.astype(jnp.bfloat16)
    taps_grad = lax.psum(taps_part, ("dp", "ctx"))
    grad_rows = jnp.where(valid_rows[:, None], back_sum, jnp.zeros_like(back_sum)).astype(
        jnp.bfloat16
    )
    grad_heads = split_heads(
        lax.all_to_all(grad_rows, "ctx", split_axis=1, concat_axis=0, tiled=True)
    )
    query_grad, key_grad, value_grad = attend_backward(
        query_heads,
        key_heads,
        value_heads,
        out_heads,
        grad_heads,
        log_totals,
        valid_keys,
        block_rows,
    )
    grads_stacked = jnp.stack(
        [
            query_grad.reshape(frames, local_width),
            key_grad.reshape(frames, local_width),
            value_grad.reshape(frames, local_width),
        ]
    )
    grads_rows = lax.all_to_all(grads_stacked, "ctx", split_axis=1, concat_axis=2, tiled=True)
    return (
        conv_out[None],
        grads_rows[0][None],
        grads_rows[1][None],
        grads_rows[2][None],
        taps_grad,
    )


def solution(mesh):
    return jax.shard_map(
        per_device,
        mesh=mesh,
        in_specs=(
            P("dp", "ctx", None),
            P("dp", "ctx", None),
            P("dp", "ctx", None),
            P("dp", "ctx", None),
            P("dp"),
            P(),
        ),
        out_specs=(
            P("dp", "ctx", None),
            P("dp", "ctx", None),
            P("dp", "ctx", None),
            P("dp", "ctx", None),
            P(),
        ),
        check_vma=False,
    )
```

profile of v0, /device:TPU:0, one launch (start us, length us, event | category | flops | bytes accessed | tf_op | source)
XLA Modules:
  0.0 237.2 jit_solution(9200691849444188628)
XLA Ops:
  8.0 1.3 collective-permute-start.2
  9.3 5.5 %collective-permute-start.3 = (bf16[15,1024]{1,0:T(8,128)(2,1)S(1)}, bf16[15,1024]{1,0:T(8,128)(2,1)S(1)}, u32[]{:S(2)}, u32[]{:S(2)}) collective-permute-start(bf16[15,1024]{1,0:T(8,128)(2,1)S(1)} %get-tuple-element.97), channel_id=1, source_target_pairs={{0,1},{1,2},{2,3},{4,5},{5,6},{6,7},{8,9},{9,10},{10,11},{12,13},{... | collective-permute-start | bytes 92168 | tf_op jit(solution)/shard_map/ppermute | solution.py:15
  14.8 1.1 fusion.144
  15.9 1.4 fusion.143
  17.9 8.8 %select_convert_fusion = bf16[128,1024]{1,0:T(8,128)(2,1)S(1)} fusion(bf16[128,1024]{1,0:T(8,128)(2,1)} %bitcast.149, bf16[15,1024]{1,0:T(8,128)(2,1)S(1)} %collective-permute-done.3, bf16[15,1024]{1,0:T(8,128)(2,1)S(1)} %collective-permute-done.2, f32[1024]{0:T(1024)S(1)} %bitcast.177, f32[1024]{0:T(1024)S(1)} %bitcast.179, f32[1024]{0:T(1024)S(1)} %bitcast.183, ...), kind=kLoop, calls=%fused_computation.214 | loop fusion | flops 24117248 | bytes 712832 | tf_op jit(solution)/shard_map/convert_element_type | solution.py:145
  27.6 4.3 %all-to-all-start.2 = ((bf16[128,4,256]{0,2,1:T(8,128)(2,1)}), bf16[128,4,256]{0,2,1:T(8,128)(2,1)S(1)}, u32[]{:S(2)}, u32[]{:S(2)}) async-start(bf16[128,4,256]{0,2,1:T(8,128)(2,1)} %bitcast.41), calls=%async_computation.2 | async-start | bytes 524288 | tf_op jit(solution)/shard_map/all_to_all | solution.py:149
  31.9 1.2 pad_maximum_fusion.1
  33.1 1.4 copy.39
  34.5 2.7 %all-to-all-done.2 = bf16[128,4,256]{0,2,1:T(8,128)(2,1)S(1)} async-done(((bf16[128,4,256]{0,2,1:T(8,128)(2,1)}), bf16[128,4,256]{0,2,1:T(8,128)(2,1)S(1)}, u32[]{:S(2)}, u32[]{:S(2)}) %all-to-all-start.2) | async-done | bytes 262176 | tf_op jit(solution)/shard_map/all_to_all | solution.py:149
  37.3 3.5 %all-to-all-start = ((bf16[3,128,1024]{1,0,2:T(4,128)(2,1)}), bf16[3,128,1024]{1,0,2:T(4,128)(2,1)S(1)}, u32[]{:S(2)}, u32[]{:S(2)}) async-start(bf16[3,128,1024]{1,0,2:T(4,128)(2,1)} %copy.39), calls=%async_computation | async-start | bytes 2097152 | tf_op jit(solution)/shard_map/all_to_all | solution.py:127
  41.1 11.9 %all-to-all-done = bf16[3,128,1024]{1,0,2:T(4,128)(2,1)S(1)} async-done(((bf16[3,128,1024]{1,0,2:T(4,128)(2,1)}), bf16[3,128,1024]{1,0,2:T(4,128)(2,1)S(1)}, u32[]{:S(2)}, u32[]{:S(2)}) %all-to-all-start) | async-done | bytes 786464 | tf_op jit(solution)/shard_map/all_to_all | solution.py:127
  54.4 1.0 fusion.1
  55.4 0.9 exponential_reduce_fusion
  57.9 1.2 multiply_reduce_fusion
  59.1 1.5 multiply_convert_fusion
  60.6 1.5 fusion.3
  62.5 2.0 copy.51
  64.5 1.0 all_to_all.51
  66.2 4.0 %all-to-all-start.1 = ((bf16[4,128,256]{1,2,0:T(8,128)(2,1)}), bf16[4,128,256]{1,2,0:T(8,128)(2,1)}, u32[]{:S(2)}, u32[]{:S(2)}) async-start(bf16[4,128,256]{1,2,0:T(8,128)(2,1)} %copy.42), calls=%async_computation.1 | async-start | bytes 524288 | tf_op jit(solution)/shard_map/all_to_all | solution.py:134
  71.2 4.5 %all-to-all-done.1 = bf16[4,128,256]{1,2,0:T(8,128)(2,1)} async-done(((bf16[4,128,256]{1,2,0:T(8,128)(2,1)}), bf16[4,128,256]{1,2,0:T(8,128)(2,1)}, u32[]{:S(2)}, u32[]{:S(2)}) %all-to-all-start.1) | async-done | bytes 262176 | tf_op jit(solution)/shard_map/all_to_all | solution.py:134
  75.7 1.1 copy.43
  76.9 3.4 %collective-permute-start = (bf16[15,1024]{1,0:T(8,128)(2,1)S(1)}, bf16[15,1024]{1,0:T(8,128)(2,1)S(1)}, u32[]{:S(2)}, u32[]{:S(2)}) collective-permute-start(bf16[15,1024]{1,0:T(8,128)(2,1)S(1)} %get-tuple-element.98), channel_id=1, source_target_pairs={{0,1},{1,2},{2,3},{4,5},{5,6},{6,7},{8,9},{9,10},{10,11},{12,13},{... | collective-permute-start | bytes 92168 | tf_op jit(solution)/shard_map/ppermute | solution.py:15
  80.3 3.8 %pad_maximum_fusion = bf16[3,512,256]{2,0,1:T(4,128)(2,1)} fusion(bf16[1,512,256]{2,0,1:T(2,128)(2,1)S(1)} %copy.52, bf16[1,512,256]{2,0,1:T(2,128)(2,1)} %copy.51, bf16[1,512,256]{2,0,1:T(2,128)(2,1)S(1)} %copy.50), kind=kLoop, calls=%fused_computation.101 | loop fusion | flops 2359296 | bytes 1572864 | tf_op jit(solution)/shard_map/stack | solution.py:161
  84.1 3.5 %all-to-all-start.3 = ((bf16[3,512,256]{2,0,1:T(4,128)(2,1)}), bf16[3,512,256]{2,0,1:T(4,128)(2,1)S(1)}, u32[]{:S(2)}, u32[]{:S(2)}) async-start(bf16[3,512,256]{2,0,1:T(4,128)(2,1)} %pad_maximum_fusion), calls=%async_computation.3 | async-start | bytes 2097152 | tf_op jit(solution)/shard_map/all_to_all | solution.py:168
  87.7 1.3 collective-permute-start.1
  90.2 9.8 %collective-permute-done.1 = bf16[15,1024]{1,0:T(8,128)(2,1)S(1)} collective-permute-done((bf16[15,1024]{1,0:T(8,128)(2,1)S(1)}, bf16[15,1024]{1,0:T(8,128)(2,1)S(1)}, u32[]{:S(2)}, u32[]{:S(2)}) %collective-permute-start.1) | collective-permute-done | bytes 30752 | tf_op jit(solution)/shard_map/ppermute | solution.py:18
  101.2 2.7 %stack.135 = f32[31,1024]{1,0:T(8,128)} concatenate(f32[1,1024]{1,0:T(1,128)S(1)} %bitcast.220, f32[1,1024]{1,0:T(1,128)S(1)} %bitcast.221, f32[1,1024]{1,0:T(1,128)S(1)} %bitcast.222, f32[1,1024]{1,0:T(1,128)S(1)} %bitcast.223, f32[1,1024]{1,0:T(1,128)S(1)} %bitcast.224, f32[1,1024]{1,0:T(1,128)S(1)} %bitcast.225, f32[1,1024]{1,0:T(1,128)S(1)} %bitcast.226, ...), dimensions={0} | concatenate | bytes 253952 | tf_op jit(solution)/shard_map/stack | solution.py:109
  103.9 3.1 %fusion.139 = bf16[1,128,1024]{2,1,0:T(8,128)(2,1)} fusion(bf16[15,1024]{1,0:T(8,128)(2,1)S(1)} %collective-permute-done.1, bf16[128,1024]{1,0:T(8,128)(2,1)S(1)} %broadcast_select_fusion, f32[1024]{0:T(1024)S(1)} %bitcast.178, f32[1024]{0:T(1024)S(1)} %bitcast.180, f32[1024]{0:T(1024)S(1)} %bitcast.184, f32[1024]{0:T(1024)S(1)} %bitcast.186, ...), kind=kLoop, calls=%fused_computation.296 | loop fusion | flops 23986176 | bytes 712704 | tf_op jit(solution)/shard_map/broadcast_in_dim | solution.py:170
  107.1 1.1 fusion.140
  109.7 0.9 slice.515
  111.8 117.0 %all-reduce.2.cloned.1.call-done = f32[31,1024]{1,0:T(8,128)} async-done(((f32[31,1024]{1,0:T(8,128)}), f32[31,1024]{1,0:T(8,128)}) %all-reduce.2.cloned.1.call-update) | async-done | bytes 126992 | tf_op jit(solution)/shard_map/psum | solution.py:144
  228.8 1.6 copy.65
  (37 shorter events, 12.2 us)
Async XLA Ops:
  8.0 10.0 %collective-permute-start.2 = (bf16[15,1024]{1,0:T(8,128)(2,1)S(1)}, bf16[15,1024]{1,0:T(8,128)(2,1)S(1)}, u32[]{:S(2)}, u32[]{:S(2)}) collective-permute-start(bf16[15,1024]{1,0:T(8,128)(2,1)S(1)} %get-tuple-element.96), channel_id=1, source_target_pairs={{1,0},{2,1},{3,2},{5,4},{6,5},{7,6},{9,8},{10,9},{11,10},{13,12},{... | collective-permute-start | bytes 92168 | tf_op jit(solution)/shard_map/ppermute | solution.py:18
  9.3 8.7 %collective-permute-start.3 = (bf16[15,1024]{1,0:T(8,128)(2,1)S(1)}, bf16[15,1024]{1,0:T(8,128)(2,1)S(1)}, u32[]{:S(2)}, u32[]{:S(2)}) collective-permute-start(bf16[15,1024]{1,0:T(8,128)(2,1)S(1)} %get-tuple-element.97), channel_id=1, source_target_pairs={{0,1},{1,2},{2,3},{4,5},{5,6},{6,7},{8,9},{9,10},{10,11},{12,13},{... | collective-permute-start | bytes 92168 | tf_op jit(solution)/shard_map/ppermute | solution.py:15
  27.6 9.7 %all-to-all-start.2 = ((bf16[128,4,256]{0,2,1:T(8,128)(2,1)}), bf16[128,4,256]{0,2,1:T(8,128)(2,1)S(1)}, u32[]{:S(2)}, u32[]{:S(2)}) async-start(bf16[128,4,256]{0,2,1:T(8,128)(2,1)} %bitcast.41), calls=%async_computation.2 | async-start | bytes 524288 | tf_op jit(solution)/shard_map/all_to_all | solution.py:149
  37.3 15.8 %all-to-all-start = ((bf16[3,128,1024]{1,0,2:T(4,128)(2,1)}), bf16[3,128,1024]{1,0,2:T(4,128)(2,1)S(1)}, u32[]{:S(2)}, u32[]{:S(2)}) async-start(bf16[3,128,1024]{1,0,2:T(4,128)(2,1)} %copy.39), calls=%async_computation | async-start | bytes 2097152 | tf_op jit(solution)/shard_map/all_to_all | solution.py:127
  66.2 9.5 %all-to-all-start.1 = ((bf16[4,128,256]{1,2,0:T(8,128)(2,1)}), bf16[4,128,256]{1,2,0:T(8,128)(2,1)}, u32[]{:S(2)}, u32[]{:S(2)}) async-start(bf16[4,128,256]{1,2,0:T(8,128)(2,1)} %copy.42), calls=%async_computation.1 | async-start | bytes 524288 | tf_op jit(solution)/shard_map/all_to_all | solution.py:134
  70.3 18.7 %copy-start = (bf16[1,128,1024]{2,1,0:T(8,128)(2,1)S(1)}, bf16[1,128,1024]{2,1,0:T(8,128)(2,1)}, u32[]{:S(2)}) copy-start(bf16[1,128,1024]{2,1,0:T(8,128)(2,1)} %param.9) | copy-start | bytes 786436
  76.9 12.1 %collective-permute-start = (bf16[15,1024]{1,0:T(8,128)(2,1)S(1)}, bf16[15,1024]{1,0:T(8,128)(2,1)S(1)}, u32[]{:S(2)}, u32[]{:S(2)}) collective-permute-start(bf16[15,1024]{1,0:T(8,128)(2,1)S(1)} %get-tuple-element.98), channel_id=1, source_target_pairs={{0,1},{1,2},{2,3},{4,5},{5,6},{6,7},{8,9},{9,10},{10,11},{12,13},{... | collective-permute-start | bytes 92168 | tf_op jit(solution)/shard_map/ppermute | solution.py:15
  84.1 23.0 %all-to-all-start.3 = ((bf16[3,512,256]{2,0,1:T(4,128)(2,1)}), bf16[3,512,256]{2,0,1:T(4,128)(2,1)S(1)}, u32[]{:S(2)}, u32[]{:S(2)}) async-start(bf16[3,512,256]{2,0,1:T(4,128)(2,1)} %pad_maximum_fusion), calls=%async_computation.3 | async-start | bytes 2097152 | tf_op jit(solution)/shard_map/all_to_all | solution.py:168
  87.6 141.2 %all-reduce.2.cloned.1.call-start = ((), (), s32[]{:S(2)}) async-start(), calls=%async_computation.4 | async-start | bytes 262144 | tf_op jit(solution)/shard_map/psum | solution.py:144
  87.7 12.3 %collective-permute-start.1 = (bf16[15,1024]{1,0:T(8,128)(2,1)S(1)}, bf16[15,1024]{1,0:T(8,128)(2,1)S(1)}, u32[]{:S(2)}, u32[]{:S(2)}) collective-permute-start(bf16[15,1024]{1,0:T(8,128)(2,1)S(1)} %get-tuple-element.99), channel_id=1, source_target_pairs={{1,0},{2,1},{3,2},{5,4},{6,5},{7,6},{9,8},{10,9},{11,10},{13,12},{... | collective-permute-start | bytes 92168 | tf_op jit(solution)/shard_map/ppermute | solution.py:18
Sparse Core Ops, SparseCore 0:
  104.0 124.7 all-reduce.1
where the time goes:
time: 238 us; the launch traced here: 237 us
  waiting for transfers between devices  146 us (61%)
  starting transfers between devices  26.8 us (11%)
  local copies, waits for them, and re-layouts  21.8 us (9%)
  other arithmetic  21.2 us (9%)
  between operations  15 us (6%)
  matrix products  6.35 us (3%)
    psum x1, waiting for transfers between devices, per_device(): taps_grad = lax.psum(taps_part, ('dp', 'ctx'))  117 us
    all_to_all x1, waiting for transfers between devices, per_device(): lax.all_to_all(stacked, 'ctx', split_axis=2, concat_axis=1, tiled=True)  11.9 us
    ppermute x2, waiting for transfers between devices, with_halo(): lax.ppermute(lax.slice_in_dim(block, 0, width, axis=dim), axis, backward)  9.84 us
    ppermute x2, starting transfers between devices, with_halo(): lax.ppermute(lax.slice_in_dim(block, block.shape[dim] - width, None, axis...  8.85 us
    convert_element_type x1, other arithmetic, per_device(): jnp.where(valid_rows[:, None], back_sum, jnp.zeros_like(back_sum))  8.83 us
  transfers between devices with their start and end apart: 9, of which 5 were waited for; matrix products, arithmetic and copies ran while one was open for 10% of the time, Pallas kernels for 0%

commit v1 on v0

--- a/solution.py
+++ b/solution.py
@@ -141,7 +141,7 @@
     padded_in = with_halo(kept, (("ctx", 0),), half_width)
     conv_sum, back_sum, taps_part = conv_terms(padded_in, padded_cot, conv_taps, tok_rows)
     conv_out = conv_sum.astype(jnp.bfloat16)
-    taps_grad = lax.psum(taps_part, ("dp", "ctx"))
+    taps_grad = lax.psum(lax.psum(taps_part, "ctx"), "dp")
     grad_rows = jnp.where(valid_rows[:, None], back_sum, jnp.zeros_like(back_sum)).astype(
         jnp.bfloat16
     )

time: 238 us -> 213 us (0.89)
  waiting for transfers between devices: 146 us -> 121 us
    psum x1 -> x2, waiting for transfers between devices: 117 us -> 91.9 us  [per_device(): taps_grad = lax.psum(lax.psum(taps_part, 'ctx'), 'dp')]
  transfers between devices with their start and end apart: 9 -> 10, of which waited for: 5 -> 6; matrix products, arithmetic and copies ran while one was open for 10% -> 11% of each run, Pallas kernels for 0% -> 0%
where the time goes in v1:
time: 213 us; the launch traced here: 212 us
  waiting for transfers between devices  121 us (57%)
  starting transfers between devices  26.9 us (13%)
  local copies, waits for them, and re-layouts  21.8 us (10%)
  other arithmetic  21.2 us (10%)
  between operations  15 us (7%)
  matrix products  6.35 us (3%)
    psum x2, waiting for transfers between devices, per_device(): taps_grad = lax.psum(lax.psum(taps_part, 'ctx'), 'dp')  91.9 us
    all_to_all x1, waiting for transfers between devices, per_device(): lax.all_to_all(stacked, 'ctx', split_axis=2, concat_axis=1, tiled=True)  11.9 us
    ppermute x2, waiting for transfers between devices, with_halo(): lax.ppermute(lax.slice_in_dim(block, 0, width, axis=dim), axis, backward)  9.84 us
    ppermute x2, starting transfers between devices, with_halo(): lax.ppermute(lax.slice_in_dim(block, block.shape[dim] - width, None, axis...  8.85 us
    convert_element_type x1, other arithmetic, per_device(): jnp.where(valid_rows[:, None], back_sum, jnp.zeros_like(back_sum))  8.83 us
    all_to_all x1, waiting for transfers between devices, per_device(): lax.all_to_all(out_heads.reshape(frames, local_width), 'ctx', split_axis=...  4.51 us
    all_to_all x1, starting transfers between devices, per_device(): lax.all_to_all(grad_rows, 'ctx', split_axis=1, concat_axis=0, tiled=True)  4.29 us
  transfers between devices with their start and end apart: 10, of which 6 were waited for; matrix products, arithmetic and copies ran while one was open for 11% of the time, Pallas kernels for 0%

profile of v1, /device:TPU:0, one launch (start us, length us, event | category | flops | bytes accessed | tf_op | source)
XLA Modules:
  0.0 212.2 jit_solution(1254793234149452821)
XLA Ops:
  8.0 1.3 collective-permute-start.2
  9.3 5.5 %collective-permute-start.3 = (bf16[15,1024]{1,0:T(8,128)(2,1)S(1)}, bf16[15,1024]{1,0:T(8,128)(2,1)S(1)}, u32[]{:S(2)}, u32[]{:S(2)}) collective-permute-start(bf16[15,1024]{1,0:T(8,128)(2,1)S(1)} %get-tuple-element.97), channel_id=1, source_target_pairs={{0,1},{1,2},{2,3},{4,5},{5,6},{6,7},{8,9},{9,10},{10,11},{12,13},{... | collective-permute-start | bytes 92168 | tf_op jit(solution)/shard_map/ppermute | solution.py:15
  14.8 1.1 fusion.144
  15.9 1.4 fusion.143
  17.9 8.8 %select_convert_fusion = bf16[128,1024]{1,0:T(8,128)(2,1)S(1)} fusion(bf16[128,1024]{1,0:T(8,128)(2,1)} %bitcast.149, bf16[15,1024]{1,0:T(8,128)(2,1)S(1)} %collective-permute-done.3, bf16[15,1024]{1,0:T(8,128)(2,1)S(1)} %collective-permute-done.2, f32[1024]{0:T(1024)S(1)} %bitcast.177, f32[1024]{0:T(1024)S(1)} %bitcast.179, f32[1024]{0:T(1024)S(1)} %bitcast.183, ...), kind=kLoop, calls=%fused_computation.214 | loop fusion | flops 24117248 | bytes 712832 | tf_op jit(solution)/shard_map/convert_element_type | solution.py:145
  27.6 4.3 %all-to-all-start.2 = ((bf16[128,4,256]{0,2,1:T(8,128)(2,1)}), bf16[128,4,256]{0,2,1:T(8,128)(2,1)S(1)}, u32[]{:S(2)}, u32[]{:S(2)}) async-start(bf16[128,4,256]{0,2,1:T(8,128)(2,1)} %bitcast.41), calls=%async_computation.2 | async-start | bytes 524288 | tf_op jit(solution)/shard_map/all_to_all | solution.py:149
  31.9 1.2 pad_maximum_fusion.1
  33.1 1.4 copy.39
  34.5 2.7 %all-to-all-done.2 = bf16[128,4,256]{0,2,1:T(8,128)(2,1)S(1)} async-done(((bf16[128,4,256]{0,2,1:T(8,128)(2,1)}), bf16[128,4,256]{0,2,1:T(8,128)(2,1)S(1)}, u32[]{:S(2)}, u32[]{:S(2)}) %all-to-all-start.2) | async-done | bytes 262176 | tf_op jit(solution)/shard_map/all_to_all | solution.py:149
  37.3 3.5 %all-to-all-start = ((bf16[3,128,1024]{1,0,2:T(4,128)(2,1)}), bf16[3,128,1024]{1,0,2:T(4,128)(2,1)S(1)}, u32[]{:S(2)}, u32[]{:S(2)}) async-start(bf16[3,128,1024]{1,0,2:T(4,128)(2,1)} %copy.39), calls=%async_computation | async-start | bytes 2097152 | tf_op jit(solution)/shard_map/all_to_all | solution.py:127
  41.1 11.9 %all-to-all-done = bf16[3,128,1024]{1,0,2:T(4,128)(2,1)S(1)} async-done(((bf16[3,128,1024]{1,0,2:T(4,128)(2,1)}), bf16[3,128,1024]{1,0,2:T(4,128)(2,1)S(1)}, u32[]{:S(2)}, u32[]{:S(2)}) %all-to-all-start) | async-done | bytes 786464 | tf_op jit(solution)/shard_map/all_to_all | solution.py:127
  54.4 1.0 fusion.1
  55.4 0.9 exponential_reduce_fusion
  57.9 1.2 multiply_reduce_fusion
  59.1 1.5 multiply_convert_fusion
  60.6 1.5 fusion.3
  62.5 2.0 copy.51
  64.5 1.0 all_to_all.51
  66.2 4.0 %all-to-all-start.1 = ((bf16[4,128,256]{1,2,0:T(8,128)(2,1)}), bf16[4,128,256]{1,2,0:T(8,128)(2,1)}, u32[]{:S(2)}, u32[]{:S(2)}) async-start(bf16[4,128,256]{1,2,0:T(8,128)(2,1)} %copy.42), calls=%async_computation.1 | async-start | bytes 524288 | tf_op jit(solution)/shard_map/all_to_all | solution.py:134
  71.2 4.5 %all-to-all-done.1 = bf16[4,128,256]{1,2,0:T(8,128)(2,1)} async-done(((bf16[4,128,256]{1,2,0:T(8,128)(2,1)}), bf16[4,128,256]{1,2,0:T(8,128)(2,1)}, u32[]{:S(2)}, u32[]{:S(2)}) %all-to-all-start.1) | async-done | bytes 262176 | tf_op jit(solution)/shard_map/all_to_all | solution.py:134
  75.7 1.1 copy.43
  76.9 3.4 %collective-permute-start = (bf16[15,1024]{1,0:T(8,128)(2,1)S(1)}, bf16[15,1024]{1,0:T(8,128)(2,1)S(1)}, u32[]{:S(2)}, u32[]{:S(2)}) collective-permute-start(bf16[15,1024]{1,0:T(8,128)(2,1)S(1)} %get-tuple-element.98), channel_id=1, source_target_pairs={{0,1},{1,2},{2,3},{4,5},{5,6},{6,7},{8,9},{9,10},{10,11},{12,13},{... | collective-permute-start | bytes 92168 | tf_op jit(solution)/shard_map/ppermute | solution.py:15
  80.3 3.8 %pad_maximum_fusion = bf16[3,512,256]{2,0,1:T(4,128)(2,1)} fusion(bf16[1,512,256]{2,0,1:T(2,128)(2,1)S(1)} %copy.52, bf16[1,512,256]{2,0,1:T(2,128)(2,1)} %copy.51, bf16[1,512,256]{2,0,1:T(2,128)(2,1)S(1)} %copy.50), kind=kLoop, calls=%fused_computation.101 | loop fusion | flops 2359296 | bytes 1572864 | tf_op jit(solution)/shard_map/stack | solution.py:161
  84.1 3.5 %all-to-all-start.3 = ((bf16[3,512,256]{2,0,1:T(4,128)(2,1)}), bf16[3,512,256]{2,0,1:T(4,128)(2,1)S(1)}, u32[]{:S(2)}, u32[]{:S(2)}) async-start(bf16[3,512,256]{2,0,1:T(4,128)(2,1)} %pad_maximum_fusion), calls=%async_computation.3 | async-start | bytes 2097152 | tf_op jit(solution)/shard_map/all_to_all | solution.py:168
  87.7 1.3 collective-permute-start.1
  90.2 9.8 %collective-permute-done.1 = bf16[15,1024]{1,0:T(8,128)(2,1)S(1)} collective-permute-done((bf16[15,1024]{1,0:T(8,128)(2,1)S(1)}, bf16[15,1024]{1,0:T(8,128)(2,1)S(1)}, u32[]{:S(2)}, u32[]{:S(2)}) %collective-permute-start.1) | collective-permute-done | bytes 30752 | tf_op jit(solution)/shard_map/ppermute | solution.py:18
  101.2 2.7 %stack.135 = f32[31,1024]{1,0:T(8,128)} concatenate(f32[1,1024]{1,0:T(1,128)S(1)} %bitcast.220, f32[1,1024]{1,0:T(1,128)S(1)} %bitcast.221, f32[1,1024]{1,0:T(1,128)S(1)} %bitcast.222, f32[1,1024]{1,0:T(1,128)S(1)} %bitcast.223, f32[1,1024]{1,0:T(1,128)S(1)} %bitcast.224, f32[1,1024]{1,0:T(1,128)S(1)} %bitcast.225, f32[1,1024]{1,0:T(1,128)S(1)} %bitcast.226, ...), dimensions={0} | concatenate | bytes 253952 | tf_op jit(solution)/shard_map/stack | solution.py:109
  104.0 3.1 %fusion.139 = bf16[1,128,1024]{2,1,0:T(8,128)(2,1)} fusion(bf16[15,1024]{1,0:T(8,128)(2,1)S(1)} %collective-permute-done.1, bf16[128,1024]{1,0:T(8,128)(2,1)S(1)} %broadcast_select_fusion, f32[1024]{0:T(1024)S(1)} %bitcast.178, f32[1024]{0:T(1024)S(1)} %bitcast.180, f32[1024]{0:T(1024)S(1)} %bitcast.184, f32[1024]{0:T(1024)S(1)} %bitcast.186, ...), kind=kLoop, calls=%fused_computation.296 | loop fusion | flops 23986176 | bytes 712704 | tf_op jit(solution)/shard_map/broadcast_in_dim | solution.py:170
  107.1 39.4 %all-reduce.3.cloned.1.call-done = f32[31,1024]{1,0:T(8,128)} async-done(((f32[31,1024]{1,0:T(8,128)}), f32[31,1024]{1,0:T(8,128)}) %all-reduce.3.cloned.1.call-update) | async-done | bytes 126992 | tf_op jit(solution)/shard_map/psum | solution.py:144
  146.6 1.1 fusion.140
  151.4 52.4 %all-reduce.5.cloned.1.call-done = f32[31,1024]{1,0:T(8,128)} async-done(((f32[31,1024]{1,0:T(8,128)}), f32[31,1024]{1,0:T(8,128)}) %all-reduce.5.cloned.1.call-update) | async-done | bytes 126992 | tf_op jit(solution)/shard_map/psum | solution.py:144
  203.8 1.6 copy.66
  (40 shorter events, 13.2 us)
Async XLA Ops:
  8.0 10.0 %collective-permute-start.2 = (bf16[15,1024]{1,0:T(8,128)(2,1)S(1)}, bf16[15,1024]{1,0:T(8,128)(2,1)S(1)}, u32[]{:S(2)}, u32[]{:S(2)}) collective-permute-start(bf16[15,1024]{1,0:T(8,128)(2,1)S(1)} %get-tuple-element.96), channel_id=1, source_target_pairs={{1,0},{2,1},{3,2},{5,4},{6,5},{7,6},{9,8},{10,9},{11,10},{13,12},{... | collective-permute-start | bytes 92168 | tf_op jit(solution)/shard_map/ppermute | solution.py:18
  9.3 8.7 %collective-permute-start.3 = (bf16[15,1024]{1,0:T(8,128)(2,1)S(1)}, bf16[15,1024]{1,0:T(8,128)(2,1)S(1)}, u32[]{:S(2)}, u32[]{:S(2)}) collective-permute-start(bf16[15,1024]{1,0:T(8,128)(2,1)S(1)} %get-tuple-element.97), channel_id=1, source_target_pairs={{0,1},{1,2},{2,3},{4,5},{5,6},{6,7},{8,9},{9,10},{10,11},{12,13},{... | collective-permute-start | bytes 92168 | tf_op jit(solution)/shard_map/ppermute | solution.py:15
  27.6 9.7 %all-to-all-start.2 = ((bf16[128,4,256]{0,2,1:T(8,128)(2,1)}), bf16[128,4,256]{0,2,1:T(8,128)(2,1)S(1)}, u32[]{:S(2)}, u32[]{:S(2)}) async-start(bf16[128,4,256]{0,2,1:T(8,128)(2,1)} %bitcast.41), calls=%async_computation.2 | async-start | bytes 524288 | tf_op jit(solution)/shard_map/all_to_all | solution.py:149
  37.3 15.8 %all-to-all-start = ((bf16[3,128,1024]{1,0,2:T(4,128)(2,1)}), bf16[3,128,1024]{1,0,2:T(4,128)(2,1)S(1)}, u32[]{:S(2)}, u32[]{:S(2)}) async-start(bf16[3,128,1024]{1,0,2:T(4,128)(2,1)} %copy.39), calls=%async_computation | async-start | bytes 2097152 | tf_op jit(solution)/shard_map/all_to_all | solution.py:127
  66.2 9.5 %all-to-all-start.1 = ((bf16[4,128,256]{1,2,0:T(8,128)(2,1)}), bf16[4,128,256]{1,2,0:T(8,128)(2,1)}, u32[]{:S(2)}, u32[]{:S(2)}) async-start(bf16[4,128,256]{1,2,0:T(8,128)(2,1)} %copy.42), calls=%async_computation.1 | async-start | bytes 524288 | tf_op jit(solution)/shard_map/all_to_all | solution.py:134
  70.3 18.7 %copy-start = (bf16[1,128,1024]{2,1,0:T(8,128)(2,1)S(1)}, bf16[1,128,1024]{2,1,0:T(8,128)(2,1)}, u32[]{:S(2)}) copy-start(bf16[1,128,1024]{2,1,0:T(8,128)(2,1)} %param.9) | copy-start | bytes 786436
  76.9 12.1 %collective-permute-start = (bf16[15,1024]{1,0:T(8,128)(2,1)S(1)}, bf16[15,1024]{1,0:T(8,128)(2,1)S(1)}, u32[]{:S(2)}, u32[]{:S(2)}) collective-permute-start(bf16[15,1024]{1,0:T(8,128)(2,1)S(1)} %get-tuple-element.98), channel_id=1, source_target_pairs={{0,1},{1,2},{2,3},{4,5},{5,6},{6,7},{8,9},{9,10},{10,11},{12,13},{... | collective-permute-start | bytes 92168 | tf_op jit(solution)/shard_map/ppermute | solution.py:15
  84.1 62.5 %all-to-all-start.3 = ((bf16[3,512,256]{2,0,1:T(4,128)(2,1)}), bf16[3,512,256]{2,0,1:T(4,128)(2,1)S(1)}, u32[]{:S(2)}, u32[]{:S(2)}) async-start(bf16[3,512,256]{2,0,1:T(4,128)(2,1)} %pad_maximum_fusion), calls=%async_computation.3 | async-start | bytes 2097152 | tf_op jit(solution)/shard_map/all_to_all | solution.py:168
  87.6 58.9 %all-reduce.3.cloned.1.call-start = ((), (), s32[]{:S(2)}) async-start(), calls=%async_computation.4 | async-start | bytes 262144 | tf_op jit(solution)/shard_map/psum | solution.py:144
  87.7 12.3 %collective-permute-start.1 = (bf16[15,1024]{1,0:T(8,128)(2,1)S(1)}, bf16[15,1024]{1,0:T(8,128)(2,1)S(1)}, u32[]{:S(2)}, u32[]{:S(2)}) collective-permute-start(bf16[15,1024]{1,0:T(8,128)(2,1)S(1)} %get-tuple-element.99), channel_id=1, source_target_pairs={{1,0},{2,1},{3,2},{5,4},{6,5},{7,6},{9,8},{10,9},{11,10},{13,12},{... | collective-permute-start | bytes 92168 | tf_op jit(solution)/shard_map/ppermute | solution.py:18
  103.9 99.9 %all-reduce.5.cloned.1.call-start = ((), (), s32[]{:S(2)}) async-start(), calls=%async_computation.5 | async-start | bytes 262144 | tf_op jit(solution)/shard_map/psum | solution.py:144
Sparse Core Ops, SparseCore 0:
  104.0 42.4 all-reduce.2
  148.9 54.8 all-reduce.4
